TPU v7x, 32 devices: a whole 2x2x4 slice. The times are simulated.
32 devices in a mesh: lag: 4 (over y, x), row: 8 (over z, core).
Axes of the slice: x: 2, y: 2, z: 4, core: 2. Of those that a mesh axis runs over, the one named last changes fastest.
Arguments:
- lag_weights: float32 [16, 4096, 4096], P('lag', 'row'), may hold values from -0.0234375 to 0.0234375
- inverse_head: float32 [4096, 4096], P('row'), may hold values from -0.09375 to 0.09375
- excitation: float32 [3, 4096, 128], P(None, 'row'), may hold values from -6 to 6
- history: float32 [16, 4096, 128], P('lag', 'row'), may hold values from -6 to 6
Outputs:
- densities: float32 [3, 4096, 128], P(None, 'row')
All inputs are finite; a program needn't handle non-finite values.
Results may differ from a plain program's by a relative error of at most 0.0001.
Values sent between devices are 32-bit elements; how exact they have to be, the bound alone decides.
No kernel may reach another device: no remote copies, remote signals or barrier semaphores. Data moves between devices by JAX's collectives and lax.ppermute only.
A program may use at most 128 MiB of HBM per device.

v0:
```python
import jax
import jax.numpy as jnp
from jax import lax
from jax.sharding import PartitionSpec as P

STEPS = 3


def from_behind(value, axis, steps):
    count = lax.axis_size(axis)
    leading, last = (max(0, -steps), min(count, count - steps))
    return lax.ppermute(value, axis, [(source, source + steps) for source in range(leading, last)])


def lag_products(weights, piece):
    return jnp.einsum("kmc,kcr->mr", weights, piece, precision=lax.Precision.HIGHEST)


def on_device(lag_weights, inverse_head, excitation, history):
    at_head = lax.axis_index("lag") == 0
    past = lax.all_gather(history, "row", axis=1, tiled=True)
    results = []
    for step in range(STEPS):
        carried = lag_products(lag_weights, past)
        carried = lax.psum(carried, "lag")
        right_side = excitation[step] - carried
        density = jnp.dot(
            inverse_head,
            lax.all_gather(right_side, "row", axis=0, tiled=True),
            precision=lax.Precision.HIGHEST,
            preferred_element_type=jnp.float32,
        )
        results.append(density)
        if step + 1 < STEPS:
            whole_density = lax.all_gather(density, "row", axis=0, tiled=True)
            moved = from_behind(past[-1], "lag", 1)
            entering = jnp.where(at_head, whole_density, moved)
            past = jnp.concatenate([entering[None], past[:-1]], axis=0)
    return jnp.stack(results, axis=0)


def solution(mesh):
    placed = (P("lag", "row", None), P("row", None), P(None, "row", None), P("lag", "row", None))
    return jax.shard_map(
        on_device, mesh=mesh, in_specs=placed, out_specs=P(None, "row", None), check_vma=False
    )
```

profile of v0, /device:TPU:0, one launch (start us, length us, event | category | flops | bytes accessed | tf_op | source)
XLA Modules:
  0.0 563.5 jit_solution(13473457763976468164)
XLA Ops:
  6.5 0.0 all-gather.7.cloned.1.call-start
  6.5 2.6 copy.5
  9.2 0.0 all-gather.7.cloned.1.call-update
  9.2 0.0 copy-start.4
  9.2 0.0 all-reduce.4.cloned.1.call-start
  9.3 84.8 %all-gather.7.cloned.1.call-done = f32[4,4096,128]{1,2,0:T(8,128)} async-done(((f32[4,512,128]{1,2,0:T(8,128)}), f32[4,4096,128]{1,2,0:T(8,128)}) %all-gather.7.cloned.1.call-update) | async-done | bytes 8388624 | tf_op jit(solution)/shard_map/all_gather | solution.py:21
  94.1 31.3 %convolution_bitcast_fusion.1 = f32[512,128]{1,0:T(8,128)} fusion(f32[4,512,4096]{2,1,0:T(8,128)} %param.4, f32[4,4096,128]{1,2,0:T(8,128)} %all-gather.7.cloned.1.call-done), kind=kOutput, calls=%fused_computation.16 | convolution fusion | flops 12884901888 | bytes 42205184 | tf_op jit(solution)/shard_map/kmc,kcr->mr/dot_general | solution.py:16
  125.4 0.0 all-reduce.4.cloned.1.call-update
  125.5 0.0 all-gather.9.cloned.1.call-start
  125.5 41.6 %all-reduce.4.cloned.1.call-done = f32[512,128]{1,0:T(8,128)} async-done(((f32[512,128]{1,0:T(8,128)}), f32[512,128]{1,0:T(8,128)}) %all-reduce.4.cloned.1.call-update) | async-done | bytes 262160 | tf_op jit(solution)/shard_map/psum | solution.py:25
  167.1 1.7 bitcast_subtract_fusion.2
  168.8 0.0 all-gather.9.cloned.1.call-update
  168.8 0.3 all-gather.11.cloned.1.call-start
  169.2 29.0 %all-gather.9.cloned.1.call-done = f32[4096,128]{1,0:T(8,128)} async-done(((f32[512,128]{1,0:T(8,128)}), f32[4096,128]{1,0:T(8,128)}) %all-gather.9.cloned.1.call-update) | async-done | bytes 2097168 | tf_op jit(solution)/shard_map/all_gather | solution.py:29
  198.1 13.5 %fusion.17 = f32[128,512]{1,0:T(8,128)} fusion(f32[4096,128]{1,0:T(8,128)} %all-gather.9.cloned.1.call-done, f32[512,4096]{1,0:T(8,128)} %param.5), kind=kOutput, calls=%fused_computation.23 | convolution fusion | flops 3221225472 | bytes 10747904 | tf_op jit(solution)/shard_map/dot_general | solution.py:27
  211.7 0.0 all-gather.11.cloned.1.call-update
  211.7 0.0 all-reduce.6.cloned.1.call-start
  211.7 4.7 slice_bitcast_fusion
  216.4 4.0 collective-permute-start
  220.4 6.2 %slice.30 = f32[3,4096,128]{1,2,0:T(8,128)} slice(f32[4,4096,128]{1,2,0:T(8,128)} %all-gather.7.cloned.1.call-done), slice={[0:3], [0:4096], [0:128]} | slice | bytes 12582912 | tf_op jit(solution)/shard_map/slice | solution.py:38
  226.6 38.7 %collective-permute-done = f32[4096,128]{0,1:T(8,128)S(1)} collective-permute-done((f32[4096,128]{0,1:T(8,128)}, f32[4096,128]{0,1:T(8,128)S(1)}, u32[]{:S(2)}, u32[]{:S(2)}) %collective-permute-start) | collective-permute-done | bytes 2097184 | tf_op jit(solution)/shard_map/ppermute | solution.py:12
  265.3 1.3 copy-done.3
  266.7 2.0 select_bitcast_fusion.1
  268.6 1.4 copy-done
  270.1 30.9 %fusion.12 = f32[512,128]{1,0:T(8,128)} fusion(f32[4,512,4096]{2,1,0:T(8,128)} %param.4, f32[3,4096,128]{1,2,0:T(8,128)S(1)} %copy-done, f32[1,4096,128]{1,2,0:T(8,128)S(1)} %select_bitcast_fusion.1), kind=kOutput, calls=%fused_computation.15 | convolution fusion | flops 12886999040 | bytes 42205184 | tf_op jit(solution)/shard_map/kmc,kcr->mr/dot_general | solution.py:16
  301.0 0.0 all-reduce.6.cloned.1.call-update
  301.0 0.0 all-gather.13.cloned.1.call-start
  301.0 43.5 %all-reduce.6.cloned.1.call-done = f32[512,128]{1,0:T(8,128)} async-done(((f32[512,128]{1,0:T(8,128)}), f32[512,128]{1,0:T(8,128)}) %all-reduce.6.cloned.1.call-update) | async-done | bytes 262160 | tf_op jit(solution)/shard_map/psum | solution.py:25
  344.5 1.7 bitcast_subtract_fusion.1
  346.2 0.0 all-gather.13.cloned.1.call-update
  346.2 0.2 all-gather.15.cloned.1.call-start
  346.4 29.1 %all-gather.13.cloned.1.call-done = f32[4096,128]{1,0:T(8,128)} async-done(((f32[512,128]{1,0:T(8,128)}), f32[4096,128]{1,0:T(8,128)}) %all-gather.13.cloned.1.call-update) | async-done | bytes 2097168 | tf_op jit(solution)/shard_map/all_gather | solution.py:29
  375.5 13.5 %fusion.18 = f32[128,512]{1,0:T(8,128)} fusion(f32[4096,128]{1,0:T(8,128)} %all-gather.13.cloned.1.call-done, f32[512,4096]{1,0:T(8,128)} %param.5), kind=kOutput, calls=%fused_computation.24 | convolution fusion | flops 3221225472 | bytes 10747904 | tf_op jit(solution)/shard_map/dot_general | solution.py:27
  389.0 0.0 all-gather.15.cloned.1.call-update
  389.1 0.0 all-reduce.8.cloned.1.call-start
  389.1 4.9 collective-permute-start.1
  394.0 44.1 %collective-permute-done.1 = f32[4096,128]{0,1:T(8,128)} collective-permute-done((f32[4096,128]{0,1:T(8,128)}, f32[4096,128]{0,1:T(8,128)}, u32[]{:S(2)}, u32[]{:S(2)}) %collective-permute-start.1) | collective-permute-done | bytes 2097184 | tf_op jit(solution)/shard_map/ppermute | solution.py:12
  438.1 1.8 select_bitcast_fusion
  439.9 31.1 %fusion.9 = f32[512,128]{1,0:T(8,128)} fusion(f32[4,512,4096]{2,1,0:T(8,128)} %param.4, f32[3,4096,128]{1,2,0:T(8,128)} %slice.30, f32[1,4096,128]{1,2,0:T(8,128)S(1)} %select_bitcast_fusion.1, f32[1,4096,128]{1,2,0:T(8,128)S(1)} %select_bitcast_fusion), kind=kOutput, calls=%fused_computation.13 | convolution fusion | flops 12889096192 | bytes 44302336 | tf_op jit(solution)/shard_map/kmc,kcr->mr/dot_general | solution.py:16
  471.0 0.0 all-reduce.8.cloned.1.call-update
  471.0 0.0 all-gather.17.cloned.1.call-start
  471.1 43.6 %all-reduce.8.cloned.1.call-done = f32[512,128]{1,0:T(8,128)} async-done(((f32[512,128]{1,0:T(8,128)}), f32[512,128]{1,0:T(8,128)}) %all-reduce.8.cloned.1.call-update) | async-done | bytes 262160 | tf_op jit(solution)/shard_map/psum | solution.py:25
  514.6 1.7 bitcast_subtract_fusion
  516.3 0.0 all-gather.17.cloned.1.call-update
  516.4 29.3 %all-gather.17.cloned.1.call-done = f32[4096,128]{1,0:T(8,128)} async-done(((f32[512,128]{1,0:T(8,128)}), f32[4096,128]{1,0:T(8,128)}) %all-gather.17.cloned.1.call-update) | async-done | bytes 2097168 | tf_op jit(solution)/shard_map/all_gather | solution.py:29
  545.7 9.9 %convolution_bitcast_fusion = f32[1,512,128]{1,2,0:T(8,128)S(1)} fusion(f32[4096,128]{1,0:T(8,128)} %all-gather.17.cloned.1.call-done, f32[512,4096]{1,0:T(8,128)} %param.5), kind=kOutput, calls=%fused_computation.14 | convolution fusion | flops 3221225472 | bytes 10747904 | tf_op jit(solution)/shard_map/dot_general | solution.py:27
  555.6 0.1 pad_maximum_fusion.1
  555.6 1.1 copy.6
  (9 shorter events, 0.0 us)
Async XLA Ops:
  6.5 87.6 %all-gather.7.cloned.1.call-start = ((), (), s32[]{:S(2)}) async-start(), calls=%async_computation | async-start | bytes 9437184 | tf_op jit(solution)/shard_map/all_gather | solution.py:21
  9.2 157.9 %copy-start.4 = (f32[3,512,128]{2,1,0:T(8,128)S(1)}, f32[3,512,128]{2,1,0:T(8,128)}, u32[]{:S(2)}) copy-start(f32[3,512,128]{2,1,0:T(8,128)} %param.6) | copy-start | bytes 2359300
  9.2 157.9 %all-reduce.4.cloned.1.call-start = ((), (), s32[]{:S(2)}) async-start(), calls=%async_computation.1 | async-start | bytes 524288 | tf_op jit(solution)/shard_map/psum | solution.py:25
  125.5 72.7 %all-gather.9.cloned.1.call-start = ((), (), s32[]{:S(2)}) async-start(), calls=%async_computation.2 | async-start | bytes 2359296 | tf_op jit(solution)/shard_map/all_gather | solution.py:29
  168.8 97.8 %all-gather.11.cloned.1.call-start = ((), (), s32[]{:S(2)}) async-start(), calls=%async_computation.3 | async-start | bytes 2359296 | tf_op jit(solution)/shard_map/all_gather | solution.py:35
  211.7 132.8 %all-reduce.6.cloned.1.call-start = ((), (), s32[]{:S(2)}) async-start(), calls=%async_computation.4 | async-start | bytes 524288 | tf_op jit(solution)/shard_map/psum | solution.py:25
  216.4 48.9 %collective-permute-start = (f32[4096,128]{0,1:T(8,128)}, f32[4096,128]{0,1:T(8,128)S(1)}, u32[]{:S(2)}, u32[]{:S(2)}) collective-permute-start(f32[4096,128]{0,1:T(8,128)} %get-tuple-element.6), channel_id=1, source_target_pairs={{0,8},{8,16},{16,24},{1,9},{9,17},{17,25},{2,10},{10,18},{18,26},{... | collective-permute-start | bytes 6291464 | tf_op jit(solution)/shard_map/ppermute | solution.py:12
  265.3 1.3 copy-start.3
  266.7 3.4 copy-start
  301.0 74.5 %all-gather.13.cloned.1.call-start = ((), (), s32[]{:S(2)}) async-start(), calls=%async_computation.5 | async-start | bytes 2359296 | tf_op jit(solution)/shard_map/all_gather | solution.py:29
  346.2 91.9 %all-gather.15.cloned.1.call-start = ((), (), s32[]{:S(2)}) async-start(), calls=%async_computation.6 | async-start | bytes 2359296 | tf_op jit(solution)/shard_map/all_gather | solution.py:35
  389.1 125.6 %all-reduce.8.cloned.1.call-start = ((), (), s32[]{:S(2)}) async-start(), calls=%async_computation.7 | async-start | bytes 524288 | tf_op jit(solution)/shard_map/psum | solution.py:25
  389.1 49.0 %collective-permute-start.1 = (f32[4096,128]{0,1:T(8,128)}, f32[4096,128]{0,1:T(8,128)}, u32[]{:S(2)}, u32[]{:S(2)}) collective-permute-start(f32[4096,128]{0,1:T(8,128)} %get-tuple-element.5), channel_id=1, source_target_pairs={{0,8},{8,16},{16,24},{1,9},{9,17},{17,25},{2,10},{10,18},{18,26},{... | collective-permute-start | bytes 6291464 | tf_op jit(solution)/shard_map/ppermute | solution.py:12
  471.0 84.5 %copy-start.1 = (f32[128,512]{1,0:T(8,128)S(1)}, f32[128,512]{1,0:T(8,128)}, u32[]{:S(2)}) copy-start(f32[128,512]{1,0:T(8,128)} %fusion.17) | copy-start | bytes 786436
  471.0 84.5 %copy-start.2 = (f32[128,512]{1,0:T(8,128)S(1)}, f32[128,512]{1,0:T(8,128)}, u32[]{:S(2)}) copy-start(f32[128,512]{1,0:T(8,128)} %fusion.18) | copy-start | bytes 786436
  471.0 74.6 %all-gather.17.cloned.1.call-start = ((), (), s32[]{:S(2)}) async-start(), calls=%async_computation.8 | async-start | bytes 2359296 | tf_op jit(solution)/shard_map/all_gather | solution.py:29
Sparse Core Ops, SparseCore 0:
  9.3 84.7 all-gather.6
  125.6 41.5 all-reduce.3
  169.0 29.1 all-gather.8
  211.8 28.5 all-gather.10
  301.1 43.3 all-reduce.5
  346.3 29.1 all-gather.12
  389.2 28.5 all-gather.14
  471.2 43.4 all-reduce.7
  516.5 29.1 all-gather.16
where the time goes:
time: 570 us; the launch traced here: 564 us
  waiting for transfers between devices  384 us (67%)
  matrix products  130 us (23%)
  local copies, waits for them, and re-layouts  17.4 us (3%)
  between operations  13.5 us (2%)
  starting transfers between devices  9.68 us (2%)
  other arithmetic  8.88 us (2%)
    psum x3, waiting for transfers between devices, on_device(): carried = lax.psum(carried, 'lag')  129 us
    dot_general x3, matrix products, lag_products(): jnp.einsum('kmc,kcr->mr', weights, piece, precision=lax.Precision.HIGHEST)  93.3 us
    all_gather x3, waiting for transfers between devices, on_device(): lax.all_gather(right_side, 'row', axis=0, tiled=True)  87.4 us
    all_gather x1, waiting for transfers between devices, on_device(): past = lax.all_gather(history, 'row', axis=1, tiled=True)  84.8 us
    ppermute x2, waiting for transfers between devices, from_behind(): lax.ppermute(value, axis, [(source, source + steps) for source in range(l...  82.8 us
    dot_general x3, matrix products, on_device(): jnp.dot(inverse_head, lax.all_gather(right_side, 'row', axis=0, tiled=Tru...  36.9 us
  transfers between devices with their start and end apart: 11, of which 9 were waited for; matrix products, arithmetic and copies ran while one was open for 2% of the time, Pallas kernels for 0%

commit v1 on v0

--- a/solution.py
+++ b/solution.py
@@ -22,7 +22,9 @@
     results = []
     for step in range(STEPS):
         carried = lag_products(lag_weights, past)
-        carried = lax.psum(carried, "lag")
+        carried = carried
+        for hop in (1, 2):
+            carried = carried + lax.ppermute(carried, "lag", [(dev, dev ^ hop) for dev in range(4)])
         right_side = excitation[step] - carried
         density = jnp.dot(
             inverse_head,

time: 570 us -> 494 us (0.87); the launches traced: 564 us -> 494 us
  waiting for transfers between devices: 384 us -> 289 us
  matrix products: 130 us -> 147 us
  starting transfers between devices: 9.68 us -> 22 us
    psum x3 -> x0, waiting for transfers between devices: 129 us -> none  [on_device(): carried = lax.psum(carried, 'lag')]
    ppermute x0 -> x6, waiting for transfers between devices: none -> 34.4 us  [on_device(): lax.ppermute(carried, 'lag', [(dev, dev ^ hop) for dev in range(4)])]
    dot_general x3, matrix products: 93.3 us -> 118 us  [lag_products(): jnp.einsum('kmc,kcr->mr', weights, piece, precision=lax.Precision.HIGHEST)]
    ppermute x0 -> x6, starting transfers between devices: none -> 13.5 us  [on_device(): lax.ppermute(carried, 'lag', [(dev, dev ^ hop) for dev in range(4)])]
    dot_general x3, matrix products: 36.9 us -> 29.5 us  [on_device(): jnp.dot(inverse_head, lax.all_gather(right_side, 'row', axis=0, tiled=Tru...]
  transfers between devices with their start and end apart: 11 -> 14, of which waited for: 9 -> 12; matrix products, arithmetic and copies ran while one was open for 2% -> 2% of each run, Pallas kernels for 0% -> 0%
where the time goes in v1:
time: 494 us
  waiting for transfers between devices  289 us (59%)
  matrix products  147 us (30%)
  starting transfers between devices  22 us (4%)
  between operations  13.6 us (3%)
  local copies, waits for them, and re-layouts  13.4 us (3%)
  other arithmetic  8.06 us (2%)
    dot_general x3, matrix products, lag_products(): jnp.einsum('kmc,kcr->mr', weights, piece, precision=lax.Precision.HIGHEST)  118 us
    all_gather x1, waiting for transfers between devices, on_device(): past = lax.all_gather(history, 'row', axis=1, tiled=True)  86.4 us
    ppermute x2, waiting for transfers between devices, from_behind(): lax.ppermute(value, axis, [(source, source + steps) for source in range(l...  83.8 us
    all_gather x3, waiting for transfers between devices, on_device(): lax.all_gather(right_side, 'row', axis=0, tiled=True)  83.7 us
    ppermute x6, waiting for transfers between devices, on_device(): lax.ppermute(carried, 'lag', [(dev, dev ^ hop) for dev in range(4)])  34.4 us
    dot_general x3, matrix products, on_device(): jnp.dot(inverse_head, lax.all_gather(right_side, 'row', axis=0, tiled=Tru...  29.5 us
    ppermute x6, starting transfers between devices, on_device(): lax.ppermute(carried, 'lag', [(dev, dev ^ hop) for dev in range(4)])  13.5 us
  transfers between devices with their start and end apart: 14, of which 12 were waited for; matrix products, arithmetic and copies ran while one was open for 2% of the time, Pallas kernels for 0%

profile of v1, /device:TPU:0, one launch (start us, length us, event | category | flops | bytes accessed | tf_op | source)
XLA Modules:
  0.0 493.5 jit_solution(16138743858741304727)
XLA Ops:
  6.5 0.7 all-gather.7.cloned.1.call-update
  7.3 0.0 all-gather.9.cloned.1.call-start
  7.3 86.4 %all-gather.7.cloned.1.call-done = f32[4,4096,128]{2,1,0:T(8,128)} async-done(((f32[4,512,128]{2,1,0:T(8,128)}), f32[4,4096,128]{2,1,0:T(8,128)}) %all-gather.7.cloned.1.call-update) | async-done | bytes 8388624 | tf_op jit(solution)/shard_map/all_gather | solution.py:21
  93.7 38.5 %convolution_bitcast_fusion.1 = f32[512,128]{1,0:T(8,128)S(1)} fusion(f32[4,512,4096]{2,1,0:T(8,128)} %param.4, f32[4,4096,128]{2,1,0:T(8,128)} %all-gather.7.cloned.1.call-done), kind=kOutput, calls=%fused_computation.16 | convolution fusion | flops 12884901888 | bytes 42205184 | tf_op jit(solution)/shard_map/kmc,kcr->mr/dot_general | solution.py:16
  132.3 1.5 collective-permute-start
  133.8 7.0 %collective-permute-done = f32[512,128]{1,0:T(8,128)S(1)} collective-permute-done((f32[512,128]{1,0:T(8,128)S(1)}, f32[512,128]{1,0:T(8,128)S(1)}, u32[]{:S(2)}, u32[]{:S(2)}) %collective-permute-start) | collective-permute-done | bytes 262176 | tf_op jit(solution)/shard_map/ppermute | solution.py:27
  140.8 1.5 collective-permute-start.1
  142.4 6.1 %collective-permute-done.1 = f32[512,128]{1,0:T(8,128)S(1)} collective-permute-done((f32[512,128]{1,0:T(8,128)S(1)}, f32[512,128]{1,0:T(8,128)S(1)}, u32[]{:S(2)}, u32[]{:S(2)}) %collective-permute-start.1) | collective-permute-done | bytes 262176 | tf_op jit(solution)/shard_map/ppermute | solution.py:27
  148.5 1.7 bitcast_subtract_fusion.2
  150.2 0.0 all-gather.9.cloned.1.call-update
  150.2 0.2 all-gather.11.cloned.1.call-start
  150.4 27.6 %all-gather.9.cloned.1.call-done = f32[4096,128]{1,0:T(8,128)} async-done(((f32[512,128]{1,0:T(8,128)}), f32[4096,128]{1,0:T(8,128)}) %all-gather.9.cloned.1.call-update) | async-done | bytes 2097168 | tf_op jit(solution)/shard_map/all_gather | solution.py:31
  178.0 10.1 %fusion.18 = f32[128,512]{0,1:T(8,128)} fusion(f32[4096,128]{1,0:T(8,128)} %all-gather.9.cloned.1.call-done, f32[512,4096]{1,0:T(8,128)} %param.5), kind=kOutput, calls=%fused_computation.24 | convolution fusion | flops 3221225472 | bytes 10747904 | tf_op jit(solution)/shard_map/dot_general | solution.py:29
  188.1 0.0 all-gather.13.cloned.1.call-start
  188.1 4.5 slice_bitcast_fusion
  192.6 3.5 collective-permute-start.2
  196.1 5.9 %slice.30 = f32[3,4096,128]{2,1,0:T(8,128)} slice(f32[4,4096,128]{2,1,0:T(8,128)} %all-gather.7.cloned.1.call-done), slice={[0:3], [0:4096], [0:128]} | slice | bytes 12582912 | tf_op jit(solution)/shard_map/slice | solution.py:40
  202.0 39.6 %collective-permute-done.2 = f32[4096,128]{1,0:T(8,128)S(1)} collective-permute-done((f32[4096,128]{1,0:T(8,128)}, f32[4096,128]{1,0:T(8,128)S(1)}, u32[]{:S(2)}, u32[]{:S(2)}) %collective-permute-start.2) | collective-permute-done | bytes 2097184 | tf_op jit(solution)/shard_map/ppermute | solution.py:12
  241.6 1.4 copy-done.3
  242.9 2.0 select_bitcast_fusion.1
  244.9 1.4 copy-done
  246.3 40.0 %fusion.12 = f32[512,128]{0,1:T(8,128)S(1)} fusion(f32[4,512,4096]{2,1,0:T(8,128)} %param.4, f32[3,4096,128]{2,1,0:T(8,128)S(1)} %copy-done, f32[1,4096,128]{2,1,0:T(8,128)S(1)} %select_bitcast_fusion.1), kind=kOutput, calls=%fused_computation.15 | convolution fusion | flops 12886999040 | bytes 42205184 | tf_op jit(solution)/shard_map/kmc,kcr->mr/dot_general | solution.py:16
  286.3 2.4 collective-permute-start.3
  288.8 5.8 %collective-permute-done.3 = f32[512,128]{0,1:T(8,128)S(1)} collective-permute-done((f32[512,128]{0,1:T(8,128)S(1)}, f32[512,128]{0,1:T(8,128)S(1)}, u32[]{:S(2)}, u32[]{:S(2)}) %collective-permute-start.3) | collective-permute-done | bytes 262176 | tf_op jit(solution)/shard_map/ppermute | solution.py:27
  294.6 2.7 collective-permute-start.4
  297.4 0.1 copy.17
  297.5 4.8 collective-permute-done.4
  302.3 0.8 bitcast_subtract_fusion.1
  303.1 0.0 all-gather.13.cloned.1.call-update
  303.1 0.0 all-gather.15.cloned.1.call-start
  303.2 28.1 %all-gather.13.cloned.1.call-done = f32[4096,128]{0,1:T(8,128)} async-done(((f32[512,128]{0,1:T(8,128)}), f32[4096,128]{0,1:T(8,128)}) %all-gather.13.cloned.1.call-update) | async-done | bytes 2097168 | tf_op jit(solution)/shard_map/all_gather | solution.py:31
  331.2 10.1 %fusion.19 = f32[128,512]{0,1:T(8,128)} fusion(f32[4096,128]{0,1:T(8,128)} %all-gather.13.cloned.1.call-done, f32[512,4096]{1,0:T(8,128)} %param.5), kind=kOutput, calls=%fused_computation.25 | convolution fusion | flops 3221225472 | bytes 10747904 | tf_op jit(solution)/shard_map/dot_general | solution.py:29
  341.3 0.0 all-gather.15.cloned.1.call-update
  341.3 0.0 all-gather.17.cloned.1.call-start
  341.4 4.7 collective-permute-start.5
  346.1 44.3 %collective-permute-done.5 = f32[4096,128]{1,0:T(8,128)} collective-permute-done((f32[4096,128]{1,0:T(8,128)}, f32[4096,128]{1,0:T(8,128)}, u32[]{:S(2)}, u32[]{:S(2)}) %collective-permute-start.5) | collective-permute-done | bytes 2097184 | tf_op jit(solution)/shard_map/ppermute | solution.py:12
  390.3 1.8 select_bitcast_fusion
  392.1 39.2 %fusion.9 = f32[512,128]{0,1:T(8,128)S(1)} fusion(f32[4,512,4096]{2,1,0:T(8,128)} %param.4, f32[3,4096,128]{2,1,0:T(8,128)} %slice.30, f32[1,4096,128]{2,1,0:T(8,128)S(1)} %select_bitcast_fusion.1, f32[1,4096,128]{2,1,0:T(8,128)S(1)} %select_bitcast_fusion), kind=kOutput, calls=%fused_computation.13 | convolution fusion | flops 12889096192 | bytes 44302336 | tf_op jit(solution)/shard_map/kmc,kcr->mr/dot_general | solution.py:16
  431.4 2.5 collective-permute-start.6
  433.9 5.8 %collective-permute-done.6 = f32[512,128]{0,1:T(8,128)S(1)} collective-permute-done((f32[512,128]{0,1:T(8,128)S(1)}, f32[512,128]{0,1:T(8,128)S(1)}, u32[]{:S(2)}, u32[]{:S(2)}) %collective-permute-start.6) | collective-permute-done | bytes 262176 | tf_op jit(solution)/shard_map/ppermute | solution.py:27
  439.8 2.7 collective-permute-start.7
  442.5 0.1 copy.18
  442.6 4.8 collective-permute-done.7
  447.5 0.8 bitcast_subtract_fusion
  448.2 0.0 all-gather.17.cloned.1.call-update
  448.3 28.1 %all-gather.17.cloned.1.call-done = f32[4096,128]{0,1:T(8,128)} async-done(((f32[512,128]{0,1:T(8,128)}), f32[4096,128]{0,1:T(8,128)}) %all-gather.17.cloned.1.call-update) | async-done | bytes 2097168 | tf_op jit(solution)/shard_map/all_gather | solution.py:31
  476.4 9.4 %convolution_bitcast_fusion = f32[1,512,128]{2,1,0:T(8,128)S(1)} fusion(f32[4096,128]{0,1:T(8,128)} %all-gather.17.cloned.1.call-done, f32[512,4096]{1,0:T(8,128)} %param.5), kind=kOutput, calls=%fused_computation.14 | convolution fusion | flops 3221225472 | bytes 10747904 | tf_op jit(solution)/shard_map/dot_general | solution.py:29
  485.8 0.9 pad_maximum_fusion.1
  (16 shorter events, 0.2 us)
Async XLA Ops:
  6.5 87.2 %all-gather.7.cloned.1.call-start = ((), (), s32[]{:S(2)}) async-start(), calls=%async_computation | async-start | bytes 9437184 | tf_op jit(solution)/shard_map/all_gather | solution.py:21
  7.3 170.8 %all-gather.9.cloned.1.call-start = ((), (), s32[]{:S(2)}) async-start(), calls=%async_computation.1 | async-start | bytes 2359296 | tf_op jit(solution)/shard_map/all_gather | solution.py:31
  132.3 8.5 %collective-permute-start = (f32[512,128]{1,0:T(8,128)S(1)}, f32[512,128]{1,0:T(8,128)S(1)}, u32[]{:S(2)}, u32[]{:S(2)}) collective-permute-start(f32[512,128]{1,0:T(8,128)S(1)} %convolution_bitcast_fusion.1), channel_id=1, source_target_pairs={{0,8},{8,0},{16,24},{24,16},{1,9},{9,1},{17,25},{25,17},{2,10},{10... | collective-permute-start | bytes 786440 | tf_op jit(solution)/shard_map/ppermute | solution.py:27
  140.8 7.7 %collective-permute-start.1 = (f32[512,128]{1,0:T(8,128)S(1)}, f32[512,128]{1,0:T(8,128)S(1)}, u32[]{:S(2)}, u32[]{:S(2)}) collective-permute-start(f32[512,128]{1,0:T(8,128)S(1)} %add.18), channel_id=1, source_target_pairs={{0,16},{8,24},{16,0},{24,8},{1,17},{9,25},{17,1},{25,9},{2,18},{10... | collective-permute-start | bytes 786440 | tf_op jit(solution)/shard_map/ppermute | solution.py:27
  150.2 92.7 %all-gather.11.cloned.1.call-start = ((), (), s32[]{:S(2)}) async-start(), calls=%async_computation.2 | async-start | bytes 2359296 | tf_op jit(solution)/shard_map/all_gather | solution.py:37
  188.1 143.1 %all-gather.13.cloned.1.call-start = ((), (), s32[]{:S(2)}) async-start(), calls=%async_computation.3 | async-start | bytes 2359296 | tf_op jit(solution)/shard_map/all_gather | solution.py:31
  192.6 48.9 %collective-permute-start.2 = (f32[4096,128]{1,0:T(8,128)}, f32[4096,128]{1,0:T(8,128)S(1)}, u32[]{:S(2)}, u32[]{:S(2)}) collective-permute-start(f32[4096,128]{1,0:T(8,128)} %get-tuple-element.6), channel_id=1, source_target_pairs={{0,8},{8,16},{16,24},{1,9},{9,17},{17,25},{2,10},{10,18},{18,26},{... | collective-permute-start | bytes 6291464 | tf_op jit(solution)/shard_map/ppermute | solution.py:12
  241.6 1.4 copy-start.3
  242.9 3.4 copy-start
  246.3 51.0 %copy-start.4 = (f32[3,512,128]{2,1,0:T(8,128)S(1)}, f32[3,512,128]{2,1,0:T(8,128)}, u32[]{:S(2)}) copy-start(f32[3,512,128]{2,1,0:T(8,128)} %param.6) | copy-start | bytes 2359300
  286.3 8.3 %collective-permute-start.3 = (f32[512,128]{0,1:T(8,128)S(1)}, f32[512,128]{0,1:T(8,128)S(1)}, u32[]{:S(2)}, u32[]{:S(2)}) collective-permute-start(f32[512,128]{0,1:T(8,128)S(1)} %fusion.12), channel_id=1, source_target_pairs={{0,8},{8,0},{16,24},{24,16},{1,9},{9,1},{17,25},{25,17},{2,10},{10... | collective-permute-start | bytes 786440 | tf_op jit(solution)/shard_map/ppermute | solution.py:27
  294.6 7.7 %collective-permute-start.4 = (f32[512,128]{0,1:T(8,128)S(1)}, f32[512,128]{0,1:T(8,128)S(1)}, u32[]{:S(2)}, u32[]{:S(2)}) collective-permute-start(f32[512,128]{0,1:T(8,128)S(1)} %add.20), channel_id=1, source_target_pairs={{0,16},{8,24},{16,0},{24,8},{1,17},{9,25},{17,1},{25,9},{2,18},{10... | collective-permute-start | bytes 786440 | tf_op jit(solution)/shard_map/ppermute | solution.py:27
  303.1 87.2 %all-gather.15.cloned.1.call-start = ((), (), s32[]{:S(2)}) async-start(), calls=%async_computation.4 | async-start | bytes 2359296 | tf_op jit(solution)/shard_map/all_gather | solution.py:37
  341.3 135.0 %all-gather.17.cloned.1.call-start = ((), (), s32[]{:S(2)}) async-start(), calls=%async_computation.5 | async-start | bytes 2359296 | tf_op jit(solution)/shard_map/all_gather | solution.py:31
  341.4 49.0 %collective-permute-start.5 = (f32[4096,128]{1,0:T(8,128)}, f32[4096,128]{1,0:T(8,128)}, u32[]{:S(2)}, u32[]{:S(2)}) collective-permute-start(f32[4096,128]{1,0:T(8,128)} %get-tuple-element.5), channel_id=1, source_target_pairs={{0,8},{8,16},{16,24},{1,9},{9,17},{17,25},{2,10},{10,18},{18,26},{... | collective-permute-start | bytes 6291464 | tf_op jit(solution)/shard_map/ppermute | solution.py:12
  431.4 8.4 %collective-permute-start.6 = (f32[512,128]{0,1:T(8,128)S(1)}, f32[512,128]{0,1:T(8,128)S(1)}, u32[]{:S(2)}, u32[]{:S(2)}) collective-permute-start(f32[512,128]{0,1:T(8,128)S(1)} %fusion.9), channel_id=1, source_target_pairs={{0,8},{8,0},{16,24},{24,16},{1,9},{9,1},{17,25},{25,17},{2,10},{10... | collective-permute-start | bytes 786440 | tf_op jit(solution)/shard_map/ppermute | solution.py:27
  439.8 7.7 %collective-permute-start.7 = (f32[512,128]{0,1:T(8,128)S(1)}, f32[512,128]{0,1:T(8,128)S(1)}, u32[]{:S(2)}, u32[]{:S(2)}) collective-permute-start(f32[512,128]{0,1:T(8,128)S(1)} %add.22), channel_id=1, source_target_pairs={{0,16},{8,24},{16,0},{24,8},{1,17},{9,25},{17,1},{25,9},{2,18},{10... | collective-permute-start | bytes 786440 | tf_op jit(solution)/shard_map/ppermute | solution.py:27
  442.5 43.2 %copy-start.1 = (f32[128,512]{0,1:T(8,128)S(1)}, f32[128,512]{0,1:T(8,128)}, u32[]{:S(2)}) copy-start(f32[128,512]{0,1:T(8,128)} %fusion.18) | copy-start | bytes 786436
  442.5 43.3 %copy-start.2 = (f32[128,512]{0,1:T(8,128)S(1)}, f32[128,512]{0,1:T(8,128)}, u32[]{:S(2)}) copy-start(f32[128,512]{0,1:T(8,128)} %fusion.19) | copy-start | bytes 786436
Sparse Core Ops, SparseCore 0:
  8.9 84.7 all-gather.6
  150.3 27.6 all-gather.8
  188.2 28.5 all-gather.10
  303.2 27.9 all-gather.12
  341.4 28.5 all-gather.14
  448.4 27.9 all-gather.16
